TPU v7x, 32 devices: a whole 2x2x4 slice. The times are simulated.
32 devices in a mesh: child: 4 (over y, x), shard: 8 (over z, core).
Axes of the slice: x: 2, y: 2, z: 4, core: 2. Of those that a mesh axis runs over, the one named last changes fastest.
Arguments:
- child_tensors: bfloat16 [4, 256, 256, 256], P('child', 'shard'), may hold values from -6 to 6
- leg_ops: bfloat16 [8, 256, 256], replicated, may hold values from -0.375 to 0.375
- term_ops: int32 [4, 4, 2], P('child'), may hold values from 0 to 7
- term_coef: float32 [4, 4], P('child'), may hold values from 0.5 to 1.5
- parent: bfloat16 [4, 256, 256], P('child', 'shard'), may hold values from -0.375 to 0.375
- top_env: float32 [256, 256], replicated, may hold values from -6 to 6
Outputs:
- applied: bfloat16 [4, 256, 256, 256], P('child', None, 'shard')
Inputs may be any that keep to these rules, and one draw needn't show every extreme that they name: `term_ops`: each entry names one of the 8 leg operators.
All inputs are finite; a program needn't handle non-finite values.
Results may differ from a plain program's by a relative error of at most 0.0091.
Values may be sent and summed in bfloat16 or wider, within the bound.
A program may use at most 128 MiB of HBM per device.

v0:
```python
import math
import jax
import jax.numpy as jnp
from jax import lax
from jax.sharding import PartitionSpec as P


def shards(child_tensors, leg_ops, term_ops, term_coef, parent, top_env):
    high = lax.Precision.HIGHEST
    tensor = child_tensors[0]
    bond = tensor.shape[1]
    picks = term_ops[0]
    weights = term_coef[0]
    number = weights.shape[0]
    onehot = (picks[:, :, None] == jnp.arange(leg_ops.shape[0])[None, None, :]).astype(jnp.bfloat16)
    chosen = jnp.einsum(
        "tjn,nab->tjab", onehot, leg_ops, preferred_element_type=jnp.float32
    ).astype(jnp.bfloat16)
    left_ops = chosen[:, 0]
    right_ops = chosen[:, 1]
    parent_block = parent[0]
    parent_full = lax.all_gather(parent_block, "shard", axis=0, tiled=True).astype(jnp.float32)
    regrouped = lax.all_to_all(tensor, "shard", split_axis=1, concat_axis=0, tiled=True)
    upward = lax.all_to_all(tensor, "shard", split_axis=2, concat_axis=0, tiled=True)
    summed = jnp.zeros((bond, bond, upward.shape[2]), jnp.float32)
    for term in range(number):
        image = jnp.einsum(
            "lru,rs->lsu", upward, right_ops[term], preferred_element_type=jnp.float32
        ).astype(jnp.bfloat16)
        summed = summed + weights[term] * jnp.einsum(
            "lk,lsu->ksu", left_ops[term], image, preferred_element_type=jnp.float32
        )
    local = lax.all_to_all(summed, "shard", split_axis=1, concat_axis=2, tiled=True)
    rounded = local.astype(jnp.bfloat16)
    env_part = (
        jnp.einsum("lsu,lsv->uv", regrouped, rounded, preferred_element_type=jnp.float32) / bond
    )
    block_rows = parent_block.astype(jnp.float32)
    env = lax.psum(env_part, "shard")
    lifted = jnp.dot(parent_full.T, jnp.dot(env, parent_full, precision=high), precision=high)
    total = lax.psum(lifted, "child")
    coupling = total - lifted + top_env
    factor = 1.0 / math.sqrt(bond * lax.axis_size("child"))
    partial_hole = (
        jnp.dot(jnp.dot(block_rows, coupling, precision=high), parent_full.T, precision=high)
        * factor
    )
    hole = lax.all_gather(partial_hole.astype(jnp.bfloat16), "shard", axis=0, tiled=True)
    result = local + jnp.einsum("lsu,uv->lsv", regrouped, hole, preferred_element_type=jnp.float32)
    return result.astype(jnp.bfloat16)[None]


def solution(mesh):
    in_specs = (
        P("child", "shard", None, None),
        P(),
        P("child", None, None),
        P("child", None),
        P("child", "shard", None),
        P(),
    )
    out_specs = P("child", None, "shard", None)
    return jax.shard_map(shards, mesh=mesh, in_specs=in_specs, out_specs=out_specs, check_vma=False)
```

profile of v0, /device:TPU:0, one launch (start us, length us, event | category | flops | bytes accessed | tf_op | source)
XLA Modules:
  0.0 548.4 jit_solution(6958713158814415964)
XLA Ops:
  6.5 8.0 %copy.56 = bf16[1,32,256,256]{2,1,3,0:T(8,128)(2,1)} copy(bf16[1,32,256,256]{3,2,1,0:T(8,128)(2,1)} %param.6) | data formatting | bytes 8388608 | tf_op args[0]
  14.5 6.4 %all-to-all-start = ((bf16[32,256,256]{1,0,2:T(8,128)(2,1)}), bf16[32,256,256]{1,0,2:T(8,128)(2,1)}, u32[]{:S(2)}, u32[]{:S(2)}) async-start(bf16[32,256,256]{1,0,2:T(8,128)(2,1)} %bitcast.131), calls=%async_computation | async-start | bytes 8388608 | tf_op jit(solution)/shard_map/all_to_all | solution.py:24
  20.9 6.6 %copy.78 = bf16[32,256,256]{2,0,1:T(8,128)(2,1)} copy(bf16[32,256,256]{2,1,0:T(8,128)(2,1)} %bitcast.130) | data formatting | bytes 8388608 | tf_op jit(solution)/shard_map/squeeze | solution.py:10
  27.4 87.5 %all-to-all-done = bf16[32,256,256]{1,0,2:T(8,128)(2,1)} async-done(((bf16[32,256,256]{1,0,2:T(8,128)(2,1)}), bf16[32,256,256]{1,0,2:T(8,128)(2,1)}, u32[]{:S(2)}, u32[]{:S(2)}) %all-to-all-start) | async-done | bytes 4194336 | tf_op jit(solution)/shard_map/all_to_all | solution.py:24
  114.9 4.6 all-to-all-start.2
  119.6 0.9 convolution_convert_fusion
  120.4 0.0 copy-start.5
  120.4 1.7 fusion.61
  122.2 0.1 copy.101
  122.3 0.1 copy.102
  122.5 0.1 copy.100
  122.6 0.1 copy.99
  122.8 0.1 copy.96
  122.9 0.1 copy.97
  123.1 0.1 copy.103
  123.2 0.1 copy.104
  123.4 0.7 fusion.62
  124.0 6.7 %copy.58 = bf16[8,32,256,32]{2,3,1,0:T(8,128)(2,1)} copy(bf16[8,32,256,32]{2,1,3,0:T(8,128)(2,1)} %bitcast.12) | data formatting | bytes 8388608 | tf_op jit(solution)/shard_map/all_to_all | solution.py:24
  130.7 9.6 %fusion.3 = f32[256,256,32]{1,0,2:T(8,128)} fusion(bf16[256,256,32]{1,2,0:T(8,128)(2,1)} %bitcast.126, bf16[1,1,256,256]{2,3,1,0:T(8,128)(2,1)S(1)} %copy.102, bf16[1,1,256,256]{2,3,1,0:T(8,128)(2,1)S(1)} %copy.101), kind=kOutput, calls=%fused_computation.5 | convolution fusion | flops 2149580800 | bytes 12845056 | tf_op jit(solution)/shard_map/lk,lsu->ksu/dot_general | solution.py:30
  140.3 9.6 %fusion.5 = f32[256,256,32]{1,0,2:T(8,128)} fusion(bf16[256,256,32]{1,2,0:T(8,128)(2,1)} %bitcast.127, bf16[1,1,256,256]{2,3,1,0:T(8,128)(2,1)S(1)} %copy.100, bf16[1,1,256,256]{2,3,1,0:T(8,128)(2,1)S(1)} %copy.99), kind=kOutput, calls=%fused_computation.7 | convolution fusion | flops 2149580800 | bytes 12845056 | tf_op jit(solution)/shard_map/lk,lsu->ksu/dot_general | solution.py:30
  149.9 9.9 %fusion.7 = f32[256,256,32]{1,0,2:T(8,128)} fusion(bf16[256,256,32]{1,2,0:T(8,128)(2,1)} %bitcast.128, bf16[1,1,256,256]{2,3,1,0:T(8,128)(2,1)S(1)} %copy.97, bf16[1,1,256,256]{2,3,1,0:T(8,128)(2,1)S(1)} %copy.96), kind=kOutput, calls=%fused_computation.9 | convolution fusion | flops 2149580800 | bytes 12845056 | tf_op jit(solution)/shard_map/lk,lsu->ksu/dot_general | solution.py:30
  159.8 19.6 %multiply_add_fusion = f32[256,256,32]{1,0,2:T(8,128)} fusion(f32[256,256,32]{1,0,2:T(8,128)} %fusion.3, f32[256,256,32]{1,0,2:T(8,128)} %fusion.5, f32[256,256,32]{1,0,2:T(8,128)} %fusion.7, f32[]{:T(128)} %bitcast.27, f32[]{:T(128)} %bitcast.21, f32[]{:T(128)} %bitcast.15, f32[]{:T(128)} %bitcast, bf16[256,256,32]{1,2,0:T(8,128)(2,1)} %bitcast.129, ...), kind=kOutput, calls=%fused_computation.2 | convolution fusion | flops 2164260864 | bytes 38010896 | tf_op jit(solution)/shard_map/lk,lsu->ksu/dot_general | solution.py:30
  179.4 10.3 %copy.75 = f32[256,256,32]{0,2,1:T(8,128)} copy(f32[256,256,32]{1,0,2:T(8,128)} %multiply_add_fusion) | data formatting | bytes 16777216 | tf_op jit(solution)/shard_map/add | solution.py:30
  189.7 23.8 %all-to-all-done.2 = bf16[32,256,256]{2,0,1:T(8,128)(2,1)} async-done(((bf16[32,256,256]{2,0,1:T(8,128)(2,1)}), bf16[32,256,256]{2,0,1:T(8,128)(2,1)}, u32[]{:S(2)}, u32[]{:S(2)}) %all-to-all-start.2) | async-done | bytes 4194336 | tf_op jit(solution)/shard_map/all_to_all | solution.py:23
  213.5 5.0 all-to-all-start.1
  218.5 0.0 all-reduce.3.cloned.1.call-start
  218.5 4.8 copy.80
  223.4 179.0 %all-to-all-done.1 = f32[256,256,32]{0,2,1:T(8,128)} async-done(((f32[256,256,32]{0,2,1:T(8,128)}), f32[256,256,32]{0,2,1:T(8,128)}, u32[]{:S(2)}, u32[]{:S(2)}) %all-to-all-start.1) | async-done | bytes 8388640 | tf_op jit(solution)/shard_map/all_to_all | solution.py:33
  402.3 4.0 convert_element_type.51
  406.4 0.0 copy-start
  406.4 0.5 copy.77
  406.9 1.7 copy-done
  408.6 2.0 fusion.33
  410.5 0.0 all-reduce.3.cloned.1.call-update
  410.6 0.0 all-reduce.5.cloned.1.call-start
  410.6 14.4 %all-gather = bf16[1,256,256]{2,1,0:T(8,128)(2,1)S(1)} all-gather(bf16[1,32,256]{2,1,0:T(8,128)(2,1)S(1)} %copy-done.4), channel_id=2, replica_groups=mesh['child'=4,'shard'=8] {'shard'}, dimensions={1}, use_global_device_ids=true | all-gather | bytes 147456 | tf_op jit(solution)/shard_map/all_gather | solution.py:22
  425.0 40.1 %all-reduce.3.cloned.1.call-done = f32[256,256]{0,1:T(8,128)} async-done(((f32[256,256]{0,1:T(8,128)}), f32[256,256]{0,1:T(8,128)}) %all-reduce.3.cloned.1.call-update) | async-done | bytes 262160 | tf_op jit(solution)/shard_map/psum | solution.py:39
  465.1 1.3 fusion.55
  466.4 1.1 convolution_bitcast_fusion
  467.5 0.0 all-reduce.5.cloned.1.call-update
  467.6 0.1 copy.81
  467.7 8.3 %copy.76 = f32[256,32,8,32]{0,3,2,1:T(8,128)} copy(f32[256,32,8,32]{0,3,1,2:T(8,128)} %bitcast.34) | data formatting | bytes 16777216 | tf_op jit(solution)/shard_map/all_to_all | solution.py:33
  476.0 34.1 %all-reduce.5.cloned.1.call-done = f32[256,256]{0,1:T(8,128)} async-done(((f32[256,256]{0,1:T(8,128)}), f32[256,256]{0,1:T(8,128)}) %all-reduce.5.cloned.1.call-update) | async-done | bytes 262160 | tf_op jit(solution)/shard_map/psum | solution.py:41
  510.1 1.2 fusion.37
  511.4 0.3 fusion.34
  511.6 14.1 %all_gather.7 = bf16[256,256]{1,0:T(8,128)(2,1)S(1)} all-gather(bf16[32,256]{1,0:T(8,128)(2,1)S(1)} %fusion.34), channel_id=1, replica_groups=mesh['child'=4,'shard'=8] {'shard'}, dimensions={0}, use_global_device_ids=true | all-gather | bytes 147456 | tf_op jit(solution)/shard_map/all_gather | solution.py:48
  525.7 8.0 %fusion.31 = bf16[1,256,32,256]{1,3,2,0:T(8,128)(2,1)} fusion(bf16[256,32,256]{2,0,1:T(8,128)(2,1)} %bitcast.132, f32[256,32,8,32]{0,3,2,1:T(8,128)} %copy.76, bf16[256,256]{1,0:T(8,128)(2,1)S(1)} %all_gather.7), kind=kOutput, calls=%fused_computation.23 | convolution fusion | flops 1077936128 | bytes 16908288 | tf_op jit(solution)/shard_map/lsu,uv->lsv/dot_general | solution.py:49
  533.7 7.8 %copy.82 = bf16[1,256,32,256]{3,2,1,0:T(8,128)(2,1)} copy(bf16[1,256,32,256]{1,3,2,0:T(8,128)(2,1)} %fusion.31) | data formatting | bytes 8388608 | tf_op jit(solution)/shard_map/broadcast_in_dim | solution.py:50
  (11 shorter events, 0.0 us)
Async XLA Ops:
  14.5 100.4 %all-to-all-start = ((bf16[32,256,256]{1,0,2:T(8,128)(2,1)}), bf16[32,256,256]{1,0,2:T(8,128)(2,1)}, u32[]{:S(2)}, u32[]{:S(2)}) async-start(bf16[32,256,256]{1,0,2:T(8,128)(2,1)} %bitcast.131), calls=%async_computation | async-start | bytes 8388608 | tf_op jit(solution)/shard_map/all_to_all | solution.py:24
  27.4 92.1 %copy-start.2 = (bf16[8,256,256]{2,1,0:T(8,128)(2,1)S(1)}, bf16[8,256,256]{2,1,0:T(8,128)(2,1)}, u32[]{:S(2)}) copy-start(bf16[8,256,256]{2,1,0:T(8,128)(2,1)} %param.7) | copy-start | bytes 3145732
  27.4 92.1 %copy-start.6 = (s32[1,4,2]{1,2,0:T(2,128)S(1)}, s32[1,4,2]{1,2,0:T(2,128)}, u32[]{:S(2)}) copy-start(s32[1,4,2]{1,2,0:T(2,128)} %param.8) | copy-start | bytes 100
  114.9 98.6 %all-to-all-start.2 = ((bf16[32,256,256]{2,0,1:T(8,128)(2,1)}), bf16[32,256,256]{2,0,1:T(8,128)(2,1)}, u32[]{:S(2)}, u32[]{:S(2)}) async-start(bf16[32,256,256]{2,0,1:T(8,128)(2,1)} %copy.78), calls=%async_computation.2 | async-start | bytes 8388608 | tf_op jit(solution)/shard_map/all_to_all | solution.py:23
  120.4 2.9 copy-start.5
  213.5 188.8 %all-to-all-start.1 = ((f32[256,256,32]{0,2,1:T(8,128)}), f32[256,256,32]{0,2,1:T(8,128)}, u32[]{:S(2)}, u32[]{:S(2)}) async-start(f32[256,256,32]{0,2,1:T(8,128)} %copy.75), calls=%async_computation.1 | async-start | bytes 16777216 | tf_op jit(solution)/shard_map/all_to_all | solution.py:33
  218.5 246.6 %all-reduce.3.cloned.1.call-start = ((), (), s32[]{:S(2)}) async-start(), calls=%async_computation.3 | async-start | bytes 524288 | tf_op jit(solution)/shard_map/psum | solution.py:39
  406.4 2.2 copy-start
  408.6 2.1 copy-start.4
  408.6 59.0 %copy-start.3 = (f32[256,256]{1,0:T(8,128)S(1)}, f32[256,256]{1,0:T(8,128)}, u32[]{:S(2)}) copy-start(f32[256,256]{1,0:T(8,128)} %param.11) | copy-start | bytes 786436
  410.6 99.6 %all-reduce.5.cloned.1.call-start = ((), (), s32[]{:S(2)}) async-start(), calls=%async_computation.4 | async-start | bytes 524288 | tf_op jit(solution)/shard_map/psum | solution.py:41
  467.7 42.4 %copy-start.1 = (f32[256,256]{0,1:T(8,128)S(1)}, f32[256,256]{0,1:T(8,128)}, u32[]{:S(2)}) copy-start(f32[256,256]{0,1:T(8,128)} %convolution_bitcast_fusion) | copy-start | bytes 786436
Sparse Core Ops, SparseCore 0:
  410.7 54.3 all-reduce.2
  468.0 42.0 all-reduce.4
where the time goes:
time: 550 us; the launch traced here: 548 us
  waiting for transfers between devices  364 us (66%)
  matrix products  63.5 us (12%)
  local copies, waits for them, and re-layouts  58.4 us (11%)
  blocking collectives  28.4 us (5%)
  starting transfers between devices  16 us (3%)
  between operations  13.6 us (2%)
    all_to_all x1, waiting for transfers between devices, shards(): lax.all_to_all(summed, 'shard', split_axis=1, concat_axis=2, tiled=True)  179 us
    all_to_all x1, waiting for transfers between devices, shards(): lax.all_to_all(tensor, 'shard', split_axis=2, concat_axis=0, tiled=True)  87.5 us
    dot_general x4, matrix products, shards(): jnp.einsum('lk,lsu->ksu', left_ops[term], image, preferred_element_type=j...  48.7 us
    psum x1, waiting for transfers between devices, shards(): env = lax.psum(env_part, 'shard')  40.1 us
    psum x1, waiting for transfers between devices, shards(): total = lax.psum(lifted, 'child')  34.1 us
    all_to_all x1, waiting for transfers between devices, shards(): lax.all_to_all(tensor, 'shard', split_axis=1, concat_axis=0, tiled=True)  23.8 us
    all_gather x1, blocking collectives, shards(): lax.all_gather(parent_block, 'shard', axis=0, tiled=True)  14.4 us
    all_gather x1, blocking collectives, shards(): lax.all_gather(partial_hole.astype(jnp.bfloat16), 'shard', axis=0, tiled=...  14.1 us
  transfers between devices with their start and end apart: 5, of which 5 were waited for; matrix products, arithmetic and copies ran while one was open for 16% of the time, Pallas kernels for 0%

commit v1 on v0

--- a/solution.py
+++ b/solution.py
@@ -38,7 +38,7 @@
     block_rows = parent_block.astype(jnp.float32)
     env = lax.psum(env_part, "shard")
     lifted = jnp.dot(parent_full.T, jnp.dot(env, parent_full, precision=high), precision=high)
-    total = lax.psum(lifted, "child")
+    total = jnp.sum(lax.all_gather(lifted, "child"), axis=0)
     coupling = total - lifted + top_env
     factor = 1.0 / math.sqrt(bond * lax.axis_size("child"))
     partial_hole = (

time: 550 us -> 534 us (0.971)
  waiting for transfers between devices: 364 us -> 347 us
    psum x1 -> x0, waiting for transfers between devices: 34.1 us -> none  [shards(): total = lax.psum(lifted, 'child')]
    all_gather x0 -> x1, waiting for transfers between devices: none -> 17.1 us  [shards(): total = jnp.sum(lax.all_gather(lifted, 'child'), axis=0)]
  transfers between devices with their start and end apart: 5 -> 5, of which waited for: 5 -> 5; matrix products, arithmetic and copies ran while one was open for 16% -> 17% of each run, Pallas kernels for 0% -> 0%
where the time goes in v1:
time: 534 us; the launch traced here: 533 us
  waiting for transfers between devices  347 us (65%)
  matrix products  62.5 us (12%)
  local copies, waits for them, and re-layouts  60.1 us (11%)
  blocking collectives  28.4 us (5%)
  starting transfers between devices  16 us (3%)
  between operations  13.6 us (3%)
    all_to_all x1, waiting for transfers between devices, shards(): lax.all_to_all(summed, 'shard', split_axis=1, concat_axis=2, tiled=True)  179 us
    all_to_all x1, waiting for transfers between devices, shards(): lax.all_to_all(tensor, 'shard', split_axis=2, concat_axis=0, tiled=True)  87.5 us
    dot_general x4, matrix products, shards(): jnp.einsum('lk,lsu->ksu', left_ops[term], image, preferred_element_type=j...  48.7 us
    psum x1, waiting for transfers between devices, shards(): env = lax.psum(env_part, 'shard')  40.1 us
    all_to_all x1, waiting for transfers between devices, shards(): lax.all_to_all(tensor, 'shard', split_axis=1, concat_axis=0, tiled=True)  23.8 us
    all_gather x1, waiting for transfers between devices, shards(): total = jnp.sum(lax.all_gather(lifted, 'child'), axis=0)  17.1 us
    all_gather x1, blocking collectives, shards(): lax.all_gather(parent_block, 'shard', axis=0, tiled=True)  14.4 us
    all_gather x1, blocking collectives, shards(): lax.all_gather(partial_hole.astype(jnp.bfloat16), 'shard', axis=0, tiled=...  14.1 us
  transfers between devices with their start and end apart: 5, of which 5 were waited for; matrix products, arithmetic and copies ran while one was open for 17% of the time, Pallas kernels for 0%

profile of v1, /device:TPU:0, one launch (start us, length us, event | category | flops | bytes accessed | tf_op | source)
XLA Modules:
  0.0 532.8 jit_solution(16333844639123428774)
XLA Ops:
  6.5 8.0 %copy.56 = bf16[1,32,256,256]{2,1,3,0:T(8,128)(2,1)} copy(bf16[1,32,256,256]{3,2,1,0:T(8,128)(2,1)} %param.6) | data formatting | bytes 8388608 | tf_op args[0]
  14.5 6.4 %all-to-all-start = ((bf16[32,256,256]{1,0,2:T(8,128)(2,1)}), bf16[32,256,256]{1,0,2:T(8,128)(2,1)}, u32[]{:S(2)}, u32[]{:S(2)}) async-start(bf16[32,256,256]{1,0,2:T(8,128)(2,1)} %bitcast.133), calls=%async_computation | async-start | bytes 8388608 | tf_op jit(solution)/shard_map/all_to_all | solution.py:24
  20.9 6.6 %copy.78 = bf16[32,256,256]{2,0,1:T(8,128)(2,1)} copy(bf16[32,256,256]{2,1,0:T(8,128)(2,1)} %bitcast.132) | data formatting | bytes 8388608 | tf_op jit(solution)/shard_map/squeeze | solution.py:10
  27.4 87.5 %all-to-all-done = bf16[32,256,256]{1,0,2:T(8,128)(2,1)} async-done(((bf16[32,256,256]{1,0,2:T(8,128)(2,1)}), bf16[32,256,256]{1,0,2:T(8,128)(2,1)}, u32[]{:S(2)}, u32[]{:S(2)}) %all-to-all-start) | async-done | bytes 4194336 | tf_op jit(solution)/shard_map/all_to_all | solution.py:24
  114.9 4.6 all-to-all-start.2
  119.6 0.9 convolution_convert_fusion
  120.4 1.7 fusion.61
  122.2 0.1 copy.101
  122.3 0.1 copy.102
  122.5 0.1 copy.100
  122.6 0.1 copy.99
  122.8 0.1 copy.96
  122.9 0.1 copy.97
  123.1 0.1 copy.103
  123.2 0.1 copy.104
  123.4 0.7 fusion.62
  124.0 6.7 %copy.58 = bf16[8,32,256,32]{2,3,1,0:T(8,128)(2,1)} copy(bf16[8,32,256,32]{2,1,3,0:T(8,128)(2,1)} %bitcast.12) | data formatting | bytes 8388608 | tf_op jit(solution)/shard_map/all_to_all | solution.py:24
  130.7 9.6 %fusion.3 = f32[256,256,32]{1,0,2:T(8,128)} fusion(bf16[256,256,32]{1,2,0:T(8,128)(2,1)} %bitcast.128, bf16[1,1,256,256]{2,3,1,0:T(8,128)(2,1)S(1)} %copy.102, bf16[1,1,256,256]{2,3,1,0:T(8,128)(2,1)S(1)} %copy.101), kind=kOutput, calls=%fused_computation.5 | convolution fusion | flops 2149580800 | bytes 12845056 | tf_op jit(solution)/shard_map/lk,lsu->ksu/dot_general | solution.py:30
  140.3 9.6 %fusion.5 = f32[256,256,32]{1,0,2:T(8,128)} fusion(bf16[256,256,32]{1,2,0:T(8,128)(2,1)} %bitcast.129, bf16[1,1,256,256]{2,3,1,0:T(8,128)(2,1)S(1)} %copy.100, bf16[1,1,256,256]{2,3,1,0:T(8,128)(2,1)S(1)} %copy.99), kind=kOutput, calls=%fused_computation.7 | convolution fusion | flops 2149580800 | bytes 12845056 | tf_op jit(solution)/shard_map/lk,lsu->ksu/dot_general | solution.py:30
  149.9 9.9 %fusion.7 = f32[256,256,32]{1,0,2:T(8,128)} fusion(bf16[256,256,32]{1,2,0:T(8,128)(2,1)} %bitcast.130, bf16[1,1,256,256]{2,3,1,0:T(8,128)(2,1)S(1)} %copy.97, bf16[1,1,256,256]{2,3,1,0:T(8,128)(2,1)S(1)} %copy.96), kind=kOutput, calls=%fused_computation.9 | convolution fusion | flops 2149580800 | bytes 12845056 | tf_op jit(solution)/shard_map/lk,lsu->ksu/dot_general | solution.py:30
  159.8 19.6 %multiply_add_fusion = f32[256,256,32]{1,0,2:T(8,128)} fusion(f32[256,256,32]{1,0,2:T(8,128)} %fusion.3, f32[256,256,32]{1,0,2:T(8,128)} %fusion.5, f32[256,256,32]{1,0,2:T(8,128)} %fusion.7, f32[]{:T(128)} %bitcast.27, f32[]{:T(128)} %bitcast.21, f32[]{:T(128)} %bitcast.15, f32[]{:T(128)} %bitcast, bf16[256,256,32]{1,2,0:T(8,128)(2,1)} %bitcast.131, ...), kind=kOutput, calls=%fused_computation.2 | convolution fusion | flops 2164260864 | bytes 38010896 | tf_op jit(solution)/shard_map/lk,lsu->ksu/dot_general | solution.py:30
  179.4 10.3 %copy.75 = f32[256,256,32]{0,2,1:T(8,128)} copy(f32[256,256,32]{1,0,2:T(8,128)} %multiply_add_fusion) | data formatting | bytes 16777216 | tf_op jit(solution)/shard_map/add | solution.py:30
  189.7 23.8 %all-to-all-done.2 = bf16[32,256,256]{2,0,1:T(8,128)(2,1)} async-done(((bf16[32,256,256]{2,0,1:T(8,128)(2,1)}), bf16[32,256,256]{2,0,1:T(8,128)(2,1)}, u32[]{:S(2)}, u32[]{:S(2)}) %all-to-all-start.2) | async-done | bytes 4194336 | tf_op jit(solution)/shard_map/all_to_all | solution.py:23
  213.5 5.0 all-to-all-start.1
  218.5 0.0 all-reduce.2.cloned.1.call-start
  218.5 4.8 copy.80
  223.4 179.0 %all-to-all-done.1 = f32[256,256,32]{0,2,1:T(8,128)} async-done(((f32[256,256,32]{0,2,1:T(8,128)}), f32[256,256,32]{0,2,1:T(8,128)}, u32[]{:S(2)}, u32[]{:S(2)}) %all-to-all-start.1) | async-done | bytes 8388640 | tf_op jit(solution)/shard_map/all_to_all | solution.py:33
  402.3 4.0 convert_element_type.51
  406.4 0.5 copy.77
  406.9 1.7 copy-done
  408.6 2.0 fusion.33
  410.5 0.0 all-reduce.2.cloned.1.call-update
  410.6 0.0 all-gather.4.cloned.1.call-start
  410.6 14.4 %all-gather = bf16[1,256,256]{2,1,0:T(8,128)(2,1)S(1)} all-gather(bf16[1,32,256]{2,1,0:T(8,128)(2,1)S(1)} %copy-done.4), channel_id=2, replica_groups=mesh['child'=4,'shard'=8] {'shard'}, dimensions={1}, use_global_device_ids=true | all-gather | bytes 147456 | tf_op jit(solution)/shard_map/all_gather | solution.py:22
  425.0 40.1 %all-reduce.2.cloned.1.call-done = f32[256,256]{0,1:T(8,128)} async-done(((f32[256,256]{0,1:T(8,128)}), f32[256,256]{0,1:T(8,128)}) %all-reduce.2.cloned.1.call-update) | async-done | bytes 262160 | tf_op jit(solution)/shard_map/psum | solution.py:39
  465.1 1.3 fusion.55
  466.4 1.1 convolution_bitcast_fusion
  467.5 0.0 all-gather.4.cloned.1.call-update
  467.6 0.1 copy.81
  467.7 8.3 %copy.76 = f32[256,32,8,32]{0,3,2,1:T(8,128)} copy(f32[256,32,8,32]{0,3,1,2:T(8,128)} %bitcast.34) | data formatting | bytes 16777216 | tf_op jit(solution)/shard_map/all_to_all | solution.py:33
  476.1 17.1 %all-gather.4.cloned.1.call-done = f32[1024,256]{0,1:T(8,128)} async-done(((f32[256,256]{0,1:T(8,128)}), f32[1024,256]{0,1:T(8,128)}) %all-gather.4.cloned.1.call-update) | async-done | bytes 1048592 | tf_op jit(solution)/shard_map/all_gather | solution.py:41
  493.1 1.7 reshape.27
  494.8 0.6 reduce_sum.9
  495.5 0.3 fusion.37
  495.7 0.3 fusion.34
  496.0 14.1 %all_gather.15 = bf16[256,256]{1,0:T(8,128)(2,1)S(1)} all-gather(bf16[32,256]{1,0:T(8,128)(2,1)S(1)} %fusion.34), channel_id=1, replica_groups=mesh['child'=4,'shard'=8] {'shard'}, dimensions={0}, use_global_device_ids=true | all-gather | bytes 147456 | tf_op jit(solution)/shard_map/all_gather | solution.py:48
  510.1 8.0 %fusion.31 = bf16[1,256,32,256]{1,3,2,0:T(8,128)(2,1)} fusion(bf16[256,32,256]{2,0,1:T(8,128)(2,1)} %bitcast.134, f32[256,32,8,32]{0,3,2,1:T(8,128)} %copy.76, bf16[256,256]{1,0:T(8,128)(2,1)S(1)} %all_gather.15), kind=kOutput, calls=%fused_computation.23 | convolution fusion | flops 1077936128 | bytes 16908288 | tf_op jit(solution)/shard_map/lsu,uv->lsv/dot_general | solution.py:49
  518.1 7.8 %copy.82 = bf16[1,256,32,256]{3,2,1,0:T(8,128)(2,1)} copy(bf16[1,256,32,256]{1,3,2,0:T(8,128)(2,1)} %fusion.31) | data formatting | bytes 8388608 | tf_op jit(solution)/shard_map/broadcast_in_dim | solution.py:50
  (13 shorter events, 0.0 us)
Async XLA Ops:
  14.5 100.4 %all-to-all-start = ((bf16[32,256,256]{1,0,2:T(8,128)(2,1)}), bf16[32,256,256]{1,0,2:T(8,128)(2,1)}, u32[]{:S(2)}, u32[]{:S(2)}) async-start(bf16[32,256,256]{1,0,2:T(8,128)(2,1)} %bitcast.133), calls=%async_computation | async-start | bytes 8388608 | tf_op jit(solution)/shard_map/all_to_all | solution.py:24
  27.4 92.1 %copy-start.2 = (bf16[8,256,256]{2,1,0:T(8,128)(2,1)S(1)}, bf16[8,256,256]{2,1,0:T(8,128)(2,1)}, u32[]{:S(2)}) copy-start(bf16[8,256,256]{2,1,0:T(8,128)(2,1)} %param.7) | copy-start | bytes 3145732
  27.4 92.1 %copy-start.6 = (s32[1,4,2]{1,2,0:T(2,128)S(1)}, s32[1,4,2]{1,2,0:T(2,128)}, u32[]{:S(2)}) copy-start(s32[1,4,2]{1,2,0:T(2,128)} %param.8) | copy-start | bytes 100
  114.9 98.6 %all-to-all-start.2 = ((bf16[32,256,256]{2,0,1:T(8,128)(2,1)}), bf16[32,256,256]{2,0,1:T(8,128)(2,1)}, u32[]{:S(2)}, u32[]{:S(2)}) async-start(bf16[32,256,256]{2,0,1:T(8,128)(2,1)} %copy.78), calls=%async_computation.2 | async-start | bytes 8388608 | tf_op jit(solution)/shard_map/all_to_all | solution.py:23
  120.4 2.9 copy-start.5
  213.5 188.8 %all-to-all-start.1 = ((f32[256,256,32]{0,2,1:T(8,128)}), f32[256,256,32]{0,2,1:T(8,128)}, u32[]{:S(2)}, u32[]{:S(2)}) async-start(f32[256,256,32]{0,2,1:T(8,128)} %copy.75), calls=%async_computation.1 | async-start | bytes 16777216 | tf_op jit(solution)/shard_map/all_to_all | solution.py:33
  218.5 246.6 %all-reduce.2.cloned.1.call-start = ((), (), s32[]{:S(2)}) async-start(), calls=%async_computation.3 | async-start | bytes 524288 | tf_op jit(solution)/shard_map/psum | solution.py:39
  406.4 2.2 copy-start
  408.6 2.1 copy-start.4
  408.6 59.0 %copy-start.3 = (f32[256,256]{1,0:T(8,128)S(1)}, f32[256,256]{1,0:T(8,128)}, u32[]{:S(2)}) copy-start(f32[256,256]{1,0:T(8,128)} %param.11) | copy-start | bytes 786436
  410.6 82.6 %all-gather.4.cloned.1.call-start = ((), (), s32[]{:S(2)}) async-start(), calls=%async_computation.4 | async-start | bytes 1310720 | tf_op jit(solution)/shard_map/all_gather | solution.py:41
  467.7 27.7 %copy-start.1 = (f32[256,256]{0,1:T(8,128)S(1)}, f32[256,256]{0,1:T(8,128)}, u32[]{:S(2)}) copy-start(f32[256,256]{0,1:T(8,128)} %convolution_bitcast_fusion) | copy-start | bytes 786436
Sparse Core Ops, SparseCore 0:
  410.7 54.3 all-reduce.1
  467.7 25.4 all-gather.3
